TPU v7x, 256 devices: a whole 4x4x8 slice. The times are simulated.
256 devices in a mesh: inst: 8 (over y, x_lo), ax: 16 (over z, core), circ: 2 (over x_hi).
Axes of the slice: x: 4 (x_hi: 2, x_lo: 2; x = x_hi * 2 + x_lo), y: 4, z: 8, core: 2. Of those that a mesh axis runs over, the one named last changes fastest.
Arguments:
- flow_state: float32 [8, 7, 128, 128, 128], P('inst', None, 'ax', 'circ'), may hold values from -2 to 40, as said below
- thinc_flags: int32 [8, 128, 128], P('inst', 'ax', 'circ'), may hold values 0 or 1
Outputs:
- new_state: float32 [8, 7, 128, 128, 128], P('inst', None, 'ax', 'circ')
Inputs may be any that keep to these rules, and one draw needn't show every extreme that they name: `flow_state`: every cell holds a two-phase state with positive partial densities and positive pressure, whose seventh field, the volume fraction, lies between 0.02 and 0.98.
All inputs are finite; a program needn't handle non-finite values. No bound on the sum of `thinc_flags` on one device may be relied on, other than what follows from the above.
Results may differ from a plain program's by a relative error of at most 0.0003.
Values sent between devices are 32-bit elements; how exact they have to be, the bound alone decides.
No kernel may reach another device: no remote copies, remote signals or barrier semaphores. Data moves between devices by JAX's collectives and lax.ppermute only.
A program may use at most 64 MiB of HBM per device.

v0:
```python
import jax
import jax.numpy as jnp
from jax import lax
from jax.sharding import PartitionSpec as P

G_LIQ = 4.4
P_LIQ = 6.0
G_GAS = 1.4
BETA = 1.6
EPSA = 0.1
ALPHA = 4.0
DIAG0 = 0.016
OMEGA = 1.0
NU_T = 0.25


def extended(block, sides, width):
    for axis, dim in sides:
        count = lax.axis_size(axis)
        forward = [(i, i + 1) for i in range(count - 1)]
        forward.append((count - 1, 0))
        backward = [(target, source) for source, target in forward]
        low = lax.ppermute(
            lax.slice_in_dim(block, block.shape[dim] - width, None, axis=dim), axis, forward
        )
        high = lax.ppermute(lax.slice_in_dim(block, 0, width, axis=dim), axis, backward)
        block = jnp.concatenate([low, block, high], axis=dim)
    return block


def shifted(block, axis, distance):
    devices = range(lax.axis_size(axis))
    route = [((i - distance) % len(devices), i) for i in devices]
    return lax.ppermute(block, axis, route)


def from_behind(value, axis, by):
    devices = lax.axis_size(axis)
    pairs = [(i, i + by) for i in range(devices) if 0 <= i + by < devices]
    return lax.ppermute(value, axis, pairs)


def spectral_table(period_count):
    harmonic = jnp.arange(period_count, dtype=jnp.int32)
    phase_angle = jnp.pi / period_count * harmonic.astype(jnp.float32)
    sine_safe = jnp.where(harmonic == 0, 1.0, jnp.sin(phase_angle))
    parity = jnp.where(harmonic % 2 == 0, 1.0, -1.0)
    first_der = jnp.where(harmonic == 0, 0.0, 0.5 * parity * jnp.cos(phase_angle) / sine_safe)
    second = jnp.where(
        harmonic == 0,
        -(period_count * period_count + 2) / 12.0,
        -parity / (2.0 * sine_safe * sine_safe),
    )
    return OMEGA * first_der - NU_T * OMEGA * OMEGA * second


def table_lookup(table_values, instance_lag, period_count):
    harmonic = jnp.arange(period_count, dtype=jnp.int32)
    return jnp.sum(
        jnp.where(instance_lag[:, None] == harmonic[None, :], table_values[None, :], 0.0), axis=1
    )


def primitives(cells):
    density = cells[0] + cells[1]
    vel_ax = cells[2] / density
    vel_circ = cells[3] / density
    vel_rad = cells[4] / density
    fraction = cells[6]
    gamma_term = fraction / (G_LIQ - 1.0) + (1.0 - fraction) / (G_GAS - 1.0)
    stiff_term = fraction * (G_LIQ * P_LIQ / (G_LIQ - 1.0))
    kinetic = 0.5 * density * (vel_ax * vel_ax + vel_circ * vel_circ + vel_rad * vel_rad)
    pressure = (cells[5] - kinetic - stiff_term) / gamma_term
    sound_speed = jnp.sqrt(
        ((1.0 + 1.0 / gamma_term) * pressure + stiff_term / gamma_term) / density
    )
    return (density, vel_ax, vel_circ, pressure, sound_speed)


def sharpen(lower_val, centre, upper_val, offset):
    average = 0.5 * (lower_val + upper_val)
    difference = upper_val - lower_val
    steepness = 2.0 * (centre - average) / (jnp.abs(difference) + EPSA)
    return average + 0.5 * difference * jnp.tanh(BETA * (steepness + offset))


def physical(cells, fraction, circ_vel, pressure):
    return [
        cells[0] * circ_vel,
        cells[1] * circ_vel,
        cells[2] * circ_vel,
        cells[3] * circ_vel + pressure,
        cells[4] * circ_vel,
        (cells[5] + pressure) * circ_vel,
        fraction * circ_vel,
    ]


def face_flux(left_state, right_state, frac_left, frac_right):
    _, _, circ_left, press_left, sound_left = primitives(left_state)
    _, _, circ_right, press_right, sound_right = primitives(right_state)
    speed = jnp.maximum(jnp.abs(circ_left) + sound_left, jnp.abs(circ_right) + sound_right)
    flux_left = physical(left_state, frac_left, circ_left, press_left)
    flux_right = physical(right_state, frac_right, circ_right, press_right)
    jumps = [right_state[component] - left_state[component] for component in range(6)]
    jumps.append(frac_right - frac_left)
    return jnp.stack(
        [
            0.5 * (flux_left[component] + flux_right[component]) - 0.5 * speed * jumps[component]
            for component in range(7)
        ]
    )


def line_sweep(lower_coef, diagonal, upper_coef, right_side):

    def forward(carried, entries):
        ratio_prev, value_prev = carried
        below_coef, centre, above_coef, right_row = entries
        pivot_value = centre - below_coef * ratio_prev
        ratio_next = above_coef / pivot_value
        value_next = (right_row - below_coef[None] * value_prev) / pivot_value[None]
        return ((ratio_next, value_next), (ratio_next, value_next))

    start_state = (jnp.zeros_like(diagonal[0]), jnp.zeros_like(right_side[0]))
    _, (ratio_rows, value_rows) = lax.scan(
        forward, start_state, (lower_coef, diagonal, upper_coef, right_side)
    )

    def backward(following, entries):
        ratio_row, value_row = entries
        current = value_row - ratio_row[None] * following
        return (current, current)

    _, solved = lax.scan(
        backward, jnp.zeros_like(right_side[0]), (ratio_rows, value_rows), reverse=True
    )
    return solved


def local(flow_state, thinc_flags):
    own_slab = flow_state[0]
    period_count = lax.axis_size("inst")
    own_index = lax.axis_index("inst")
    table_values = spectral_table(period_count)
    portion = lax.all_gather(flow_state, "inst", axis=0, tiled=True)
    row_count = portion.shape[0]
    instance_lag = (own_index - jnp.arange(row_count, dtype=jnp.int32)) % period_count
    weights = table_lookup(table_values, instance_lag, period_count)
    spectral = jnp.sum(weights[:, None, None, None, None] * portion, axis=0)
    padded = extended(own_slab, (("circ", 2),), 2)
    circ_width = own_slab.shape[2]
    fraction = padded[6]
    flagged = (thinc_flags[0] > 0)[:, :, None]
    frac_back2 = fraction[:, 0:circ_width]
    frac_back1 = fraction[:, 1 : circ_width + 1]
    frac_here = fraction[:, 2 : circ_width + 2]
    frac_next = fraction[:, 3 : circ_width + 3]
    frac_left = jnp.where(flagged, sharpen(frac_back2, frac_back1, frac_here, 1.0), frac_back1)
    frac_right = jnp.where(flagged, sharpen(frac_back1, frac_here, frac_next, -1.0), frac_here)
    fluxes = face_flux(padded[:, :, 1 : circ_width + 1], own_slab, frac_left, frac_right)
    upper_flux = shifted(fluxes[:, :, 0:1], "circ", -1)
    residual = jnp.concatenate([fluxes[:, :, 1:], upper_flux], axis=2) - fluxes + spectral
    _, vel_ax, _, _, sound_speed = primitives(own_slab)
    radius = jnp.abs(vel_ax) + sound_speed
    coupling = -ALPHA * radius
    diagonal = DIAG0 + 2.0 * ALPHA * radius
    right_side = -residual
    field_count = own_slab.shape[0]
    ax_cells = own_slab.shape[1]
    interior = ax_cells - 1
    positions = jnp.arange(interior, dtype=jnp.int32)[:, None, None, None]
    plane_shape = (interior, 1) + radius.shape[1:]
    unit_first = jnp.broadcast_to((positions == 0).astype(jnp.float32), plane_shape)
    unit_last = jnp.broadcast_to((positions == interior - 1).astype(jnp.float32), plane_shape)
    stacked = jnp.concatenate(
        [jnp.swapaxes(right_side[:, :interior], 0, 1), unit_first, unit_last], axis=1
    )
    solved_local = line_sweep(
        coupling[:interior], diagonal[:interior], coupling[:interior], stacked
    )
    y_first = solved_local[0, :field_count]
    v_first = solved_local[0, field_count]
    w_first = solved_local[0, field_count + 1]
    y_last = solved_local[interior - 1, :field_count]
    v_last = solved_local[interior - 1, field_count]
    w_last = solved_local[interior - 1, field_count + 1]
    coup_first = coupling[0]
    coup_inner = coupling[interior - 1]
    coup_sep = coupling[ax_cells - 1]
    own_lower = -coup_sep * coup_first * v_last
    own_diag = diagonal[ax_cells - 1] - coup_sep * coup_inner * w_last
    own_rhs = right_side[:, ax_cells - 1] - coup_sep[None] * y_last
    give_first = coup_first * v_first
    give_last = coup_inner * w_first
    following = from_behind(
        jnp.concatenate([give_first[None], give_last[None], y_first], axis=0), "ax", -1
    )
    sep_rows = jnp.concatenate(
        [
            own_lower[None],
            (own_diag - coup_sep * following[0])[None],
            (-coup_sep * following[1])[None],
            own_rhs - coup_sep[None] * following[2:],
        ],
        axis=0,
    )
    gathered = lax.all_gather(sep_rows[None], "ax", axis=0, tiled=True)
    red_lower = gathered[:, 0]
    red_diag = gathered[:, 1]
    red_upper = gathered[:, 2]
    red_rhs = gathered[:, 3:]
    separators = line_sweep(red_lower, red_diag, red_upper, red_rhs)
    ax_index = lax.axis_index("ax")
    own_value = lax.dynamic_index_in_dim(separators, ax_index, 0, keepdims=False)
    prev_value = lax.dynamic_index_in_dim(
        separators, jnp.maximum(ax_index - 1, 0), 0, keepdims=False
    ) * (ax_index > 0).astype(jnp.float32)
    y_part = solved_local[:, :field_count]
    v_part = solved_local[:, field_count]
    w_part = solved_local[:, field_count + 1]
    interior_delta = (
        y_part
        - (coup_first[None] * v_part)[:, None] * prev_value[None]
        - (coup_inner[None] * w_part)[:, None] * own_value[None]
    )
    delta = jnp.swapaxes(jnp.concatenate([interior_delta, own_value[None]], axis=0), 0, 1)
    return (own_slab + delta)[None]


def solution(mesh):
    return jax.shard_map(
        local,
        mesh=mesh,
        in_specs=(P("inst", None, "ax", "circ", None), P("inst", "ax", "circ")),
        out_specs=P("inst", None, "ax", "circ", None),
        check_vma=False,
    )
```

profile of v0, /device:TPU:1, one launch (start us, length us, event | category | flops | bytes accessed | tf_op | source)
XLA Modules:
  0.0 523.3 jit_solution(5717942069486642746)
XLA Ops:
  8.1 3.6 collective-permute-start
  13.3 3.8 collective-permute-done.1
  19.6 1.7 slice.244
  21.8 279.9 %all-gather.4.cloned.1.call-done = f32[8,7,8,64,128]{4,3,2,1,0:T(8,128)} async-done(((f32[1,7,8,64,128]{4,3,2,1,0:T(8,128)}), f32[8,7,8,64,128]{4,3,2,1,0:T(8,128)}) %all-gather.4.cloned.1.call-update) | async-done | bytes 14680080 | tf_op jit(solution)/shard_map/all_gather | solution.py:146
  301.7 7.5 %multiply_reduce_fusion = f32[7,8,64,128]{3,2,1,0:T(8,128)S(1)} fusion(f32[8,7,8,64,128]{4,3,2,1,0:T(8,128)} %all-gather.4.cloned.1.call-done, f32[8]{0:T(128)S(1)} %select_reduce_fusion), kind=kLoop, calls=%fused_computation.25 | loop fusion | flops 6881280 | bytes 16515104 | tf_op jit(solution)/shard_map/reduce_sum | solution.py:150
  309.3 2.1 fusion.3
  315.6 16.9 %while.69 = (s32[]{:T(128)}, f32[64,128]{1,0:T(8,128)S(1)}, f32[9,64,128]{2,1,0:T(8,128)S(1)}, f32[7,64,128]{2,1,0:T(8,128)}, f32[7,9,64,128]{3,2,1,0:T(8,128)},...) while((s32[]{:T(128)}, f32[64,128]{1,0:T(8,128)S(1)}, ...), condition=%wide.region_3.4_spmd.clone, body=%wide.region_2.3_spmd.clone.sunk | while | flops 327683 | bytes 1475696 | solution.py:126
  316.2 1.8 bitcast_dynamic-update-slice_fusion.14
  318.7 1.8 bitcast_dynamic-update-slice_fusion.14
  321.1 1.8 bitcast_dynamic-update-slice_fusion.14
  323.5 1.8 bitcast_dynamic-update-slice_fusion.14
  326.0 1.8 bitcast_dynamic-update-slice_fusion.14
  328.4 1.8 bitcast_dynamic-update-slice_fusion.14
  330.8 1.8 bitcast_dynamic-update-slice_fusion.14
  334.1 18.1 %while.70 = (s32[]{:T(128)}, f32[9,64,128]{2,1,0:T(8,128)S(1)}, f32[7,9,64,128]{3,2,1,0:T(8,128)}, f32[7,9,64,128]{3,2,1,0:T(8,128)}, f32[7,64,128]{2,1,0:T(8,128)}, /*index=5*/s32[]{:T(128)}, s32[]{:T(128)}, s32[]{:T(128)}) while((s32[]{:T(128)}, f32[9,64,128]{2,1,0:T(8,128)S(1)}, f32[7,9,64,128]{3,2,1,0:T(8,128)}, ...), condition=%wide.region_5.6_spmd.clone, body=%wide.region_4.5_spmd.clone.sunk | while | flops 221188 | bytes 1278067 | solution.py:135
  334.9 1.8 bitcast_dynamic-update-slice_fusion.15
  337.5 1.8 bitcast_dynamic-update-slice_fusion.15
  340.0 1.8 bitcast_dynamic-update-slice_fusion.15
  342.6 1.8 bitcast_dynamic-update-slice_fusion.15
  345.2 1.8 bitcast_dynamic-update-slice_fusion.15
  347.7 1.8 bitcast_dynamic-update-slice_fusion.15
  350.3 1.8 bitcast_dynamic-update-slice_fusion.15
  354.0 2.7 collective-permute-start.3
  356.6 5.8 %collective-permute-done.3 = f32[9,64,128]{2,1,0:T(8,128)S(1)} collective-permute-done((f32[9,64,128]{2,1,0:T(8,128)S(1)}, f32[9,64,128]{2,1,0:T(8,128)S(1)}, u32[]{:S(2)}, u32[]{:S(2)}) %collective-permute-start.3) | collective-permute-done | bytes 294944 | tf_op jit(solution)/shard_map/ppermute | solution.py:40
  366.2 42.8 %all-gather.6.cloned.1.call-done = f32[160,64,128]{2,1,0:T(8,128)} async-done(((f32[10,64,128]{2,1,0:T(8,128)}), f32[160,64,128]{2,1,0:T(8,128)}) %all-gather.6.cloned.1.call-update) | async-done | bytes 5242896 | tf_op jit(solution)/shard_map/all_gather | solution.py:208
  409.1 4.4 slice.259
  413.4 2.5 slice_bitcast_fusion.1
  416.0 2.3 broadcast.404.clone
  418.2 49.6 %while.71 = (s32[]{:T(128)}, f32[64,128]{1,0:T(8,128)S(1)}, f32[7,64,128]{2,1,0:T(8,128)S(1)}, f32[16,64,128]{2,1,0:T(8,128)}, f32[16,7,64,128]{3,2,1,0:T(8,128)...) while((s32[]{:T(128)}, f32[64,128]{1,0:T(8,128)S(1)}, ...), condition=%wide.region_7.8_spmd.clone, body=%wide.region_6.7_spmd.clone.sunk | while | flops 262147 | bytes 1246328 | solution.py:126
  419.6 1.7 bitcast_dynamic-update-slice_fusion.17
  422.7 1.7 bitcast_dynamic-update-slice_fusion.17
  425.8 1.7 bitcast_dynamic-update-slice_fusion.17
  428.9 1.7 bitcast_dynamic-update-slice_fusion.17
  432.0 1.7 bitcast_dynamic-update-slice_fusion.17
  435.1 1.7 bitcast_dynamic-update-slice_fusion.17
  438.2 1.7 bitcast_dynamic-update-slice_fusion.17
  441.3 1.7 bitcast_dynamic-update-slice_fusion.17
  444.5 1.7 bitcast_dynamic-update-slice_fusion.17
  447.6 1.7 bitcast_dynamic-update-slice_fusion.17
  450.7 1.7 bitcast_dynamic-update-slice_fusion.17
  453.8 1.7 bitcast_dynamic-update-slice_fusion.17
  456.9 1.7 bitcast_dynamic-update-slice_fusion.17
  460.0 1.7 bitcast_dynamic-update-slice_fusion.17
  463.1 1.7 bitcast_dynamic-update-slice_fusion.17
  466.2 1.7 bitcast_dynamic-update-slice_fusion.17
  467.9 2.2 broadcast.404
  470.1 40.2 %while.72 = (s32[]{:T(128)}, f32[7,64,128]{2,1,0:T(8,128)S(1)}, f32[16,7,64,128]{3,2,1,0:T(8,128)}, f32[16,7,64,128]{3,2,1,0:T(8,128)}, f32[16,64,128]{2,1,0:T(8,128)}, /*index=5*/s32[]{:T(128)}, s32[]{:T(128)}, s32[]{:T(128)}) while((s32[]{:T(128)}, f32[7,64,128]{2,1,0:T(8,128)S(1)}, f32[16,7,64,128]{3,2,1,0:T(8,128)}, ...), condition=%wide.region_9.10_spmd.clone, body=%wide.region_8.9_spmd.clone.sunk | while | flops 172036 | bytes 1015923 | solution.py:135
  470.9 1.8 bitcast_dynamic-update-slice_fusion.18
  473.4 1.7 bitcast_dynamic-update-slice_fusion.18
  475.9 1.8 bitcast_dynamic-update-slice_fusion.18
  478.4 1.7 bitcast_dynamic-update-slice_fusion.18
  480.9 1.8 bitcast_dynamic-update-slice_fusion.18
  483.5 1.8 bitcast_dynamic-update-slice_fusion.18
  486.0 1.8 bitcast_dynamic-update-slice_fusion.18
  488.5 1.7 bitcast_dynamic-update-slice_fusion.18
  491.0 1.8 bitcast_dynamic-update-slice_fusion.18
  493.5 1.8 bitcast_dynamic-update-slice_fusion.18
  496.0 1.8 bitcast_dynamic-update-slice_fusion.18
  498.5 1.8 bitcast_dynamic-update-slice_fusion.18
  501.1 1.7 bitcast_dynamic-update-slice_fusion.18
  503.6 1.8 bitcast_dynamic-update-slice_fusion.18
  506.1 1.7 bitcast_dynamic-update-slice_fusion.18
  508.6 1.8 bitcast_dynamic-update-slice_fusion.18
  513.2 1.7 fusion.6
  (108 shorter events, 66.1 us)
Async XLA Ops:
  6.5 1.5 copy-start
  6.5 5.6 %copy-start.4 = (s32[1,8,64]{2,1,0:T(8,128)S(1)}, s32[1,8,64]{2,1,0:T(8,128)}, u32[]{:S(2)}) copy-start(s32[1,8,64]{2,1,0:T(8,128)} %param.11) | copy-start | bytes 6148
  6.5 295.2 %all-gather.4.cloned.1.call-start = ((), (), s32[]{:S(2)}) async-start(), calls=%async_computation | async-start | bytes 16515072 | tf_op jit(solution)/shard_map/all_gather | solution.py:146
  7.3 401.8 %all-gather.6.cloned.1.call-start = ((), (), s32[]{:S(2)}) async-start(), calls=%async_computation.1 | async-start | bytes 5570560 | tf_op jit(solution)/shard_map/all_gather | solution.py:208
  8.1 5.2 collective-permute-start
  11.7 5.3 %collective-permute-start.1 = (f32[7,8,2,128]{3,2,1,0:T(2,128)S(1)}, f32[7,8,2,128]{3,2,1,0:T(2,128)S(1)}, u32[]{:S(2)}, u32[]{:S(2)}) collective-permute-start(f32[7,8,2,128]{3,2,1,0:T(2,128)S(1)} %get-tuple-element.541), channel_id=1, source_target_pairs={{1,0},{0,1},{3,2},{2,3},{5,4},{4,5},{7,6},{6,7},{9,8},{8,9},{11,10... | collective-permute-start | bytes 172040 | tf_op jit(solution)/shard_map/ppermute | solution.py:26
  19.6 1.8 copy-start.1
  21.4 287.8 %collective-permute-start.2 = (f32[7,8,1,128]{3,2,1,0:T(1,128)S(1)}, f32[7,8,1,128]{3,2,1,0:T(1,128)S(1)}, u32[]{:S(2)}, u32[]{:S(2)}) collective-permute-start(f32[7,8,1,128]{3,2,1,0:T(1,128)S(1)} %slice.245), channel_id=1, source_target_pairs={{1,0},{0,1},{3,2},{2,3},{5,4},{4,5},{7,6},{6,7},{9,8},{8,9},{11,10... | collective-permute-start | bytes 86024 | tf_op jit(solution)/shard_map/ppermute | solution.py:34
  301.7 7.5 %copy-start.2 = (f32[7,8,64,128]{3,2,1,0:T(8,128)S(1)}, f32[7,8,64,128]{3,2,1,0:T(8,128)}, u32[]{:S(2)}) copy-start(f32[7,8,64,128]{3,2,1,0:T(8,128)} %copy-done.1) | copy-start | bytes 5505028
  311.4 1.2 copy-start.3
  354.0 8.5 %collective-permute-start.3 = (f32[9,64,128]{2,1,0:T(8,128)S(1)}, f32[9,64,128]{2,1,0:T(8,128)S(1)}, u32[]{:S(2)}, u32[]{:S(2)}) collective-permute-start(f32[9,64,128]{2,1,0:T(8,128)S(1)} %pad_maximum_fusion.4), channel_id=1, source_target_pairs={{2,0},{4,2},{6,4},{8,6},{10,8},{12,10},{14,12},{16,14},{18,16},{20... | collective-permute-start | bytes 884744 | tf_op jit(solution)/shard_map/ppermute | solution.py:40
Sparse Core Ops, SparseCore 0:
  9.1 292.5 all-gather.3
  365.2 43.7 all-gather.5
where the time goes:
time: 528 us; the launch traced here: 523 us
  waiting for transfers between devices  334 us (63%)
  other arithmetic  130 us (25%)
  local copies, waits for them, and re-layouts  38.7 us (7%)
  between operations  13.6 us (3%)
  starting transfers between devices  6.75 us (1%)
    all_gather x1, waiting for transfers between devices, local(): portion = lax.all_gather(flow_state, 'inst', axis=0, tiled=True)  280 us
    dynamic_update_slice x69, other arithmetic, line_sweep(): lax.scan(forward, start_state, (lower_coef, diagonal, upper_coef, right_s...  107 us
    all_gather x1, waiting for transfers between devices, local(): gathered = lax.all_gather(sep_rows[None], 'ax', axis=0, tiled=True)  42.8 us
    mul x23, local copies, waits for them, and re-layouts, backward(): current = value_row - ratio_row[None] * following  17.5 us
  transfers between devices with their start and end apart: 6, of which 5 were waited for; matrix products, arithmetic and copies ran while one was open for 3% of the time, Pallas kernels for 0%

commit v1 on v0

--- a/solution.py
+++ b/solution.py
@@ -205,7 +205,9 @@
         ],
         axis=0,
     )
-    gathered = lax.all_gather(sep_rows[None], "ax", axis=0, tiled=True)
+    gathered = jnp.concatenate(
+        lax.all_to_all(jnp.stack([sep_rows[None]] * lax.axis_size("ax")), "ax", 0, 0), axis=0
+    )
     red_lower = gathered[:, 0]
     red_diag = gathered[:, 1]
     red_upper = gathered[:, 2]

time: 528 us -> 609 us (1.15)
  waiting for transfers between devices: 334 us -> 406 us
  starting transfers between devices: 6.75 us -> 13.6 us
    all_to_all x0 -> x1, waiting for transfers between devices: none -> 115 us  [local(): lax.all_to_all(jnp.stack([sep_rows[None]] * lax.axis_size('ax')), 'ax', 0...]
    all_gather x1 -> x0, waiting for transfers between devices: 42.8 us -> none  [local(): gathered = lax.all_gather(sep_rows[None], 'ax', axis=0, tiled=True)]
    all_to_all x0 -> x1, starting transfers between devices: none -> 6.87 us  [local(): lax.all_to_all(jnp.stack([sep_rows[None]] * lax.axis_size('ax')), 'ax', 0...]
  transfers between devices with their start and end apart: 6 -> 6, of which waited for: 5 -> 5; matrix products, arithmetic and copies ran while one was open for 3% -> 2% of each run, Pallas kernels for 0% -> 0%
where the time goes in v1:
time: 609 us; the launch traced here: 605 us
  waiting for transfers between devices  406 us (67%)
  other arithmetic  130 us (21%)
  local copies, waits for them, and re-layouts  41.8 us (7%)
  starting transfers between devices  13.6 us (2%)
  between operations  13.6 us (2%)
    all_gather x1, waiting for transfers between devices, local(): portion = lax.all_gather(flow_state, 'inst', axis=0, tiled=True)  280 us
    all_to_all x1, waiting for transfers between devices, local(): lax.all_to_all(jnp.stack([sep_rows[None]] * lax.axis_size('ax')), 'ax', 0...  115 us
    dynamic_update_slice x69, other arithmetic, line_sweep(): lax.scan(forward, start_state, (lower_coef, diagonal, upper_coef, right_s...  108 us
    mul x23, local copies, waits for them, and re-layouts, backward(): current = value_row - ratio_row[None] * following  17.5 us
  transfers between devices with their start and end apart: 6, of which 5 were waited for; matrix products, arithmetic and copies ran while one was open for 2% of the time, Pallas kernels for 0%

profile of v1, /device:TPU:1, one launch (start us, length us, event | category | flops | bytes accessed | tf_op | source)
XLA Modules:
  0.0 604.8 jit_solution(7769474732519094724)
XLA Ops:
  8.1 3.6 collective-permute-start
  13.3 3.8 collective-permute-done.1
  19.6 1.7 slice.244
  21.8 279.9 %all-gather.2.cloned.1.call-done = f32[8,7,8,64,128]{4,3,2,1,0:T(8,128)} async-done(((f32[1,7,8,64,128]{4,3,2,1,0:T(8,128)}), f32[8,7,8,64,128]{4,3,2,1,0:T(8,128)}) %all-gather.2.cloned.1.call-update) | async-done | bytes 14680080 | tf_op jit(solution)/shard_map/all_gather | solution.py:146
  301.7 7.5 %multiply_reduce_fusion = f32[7,8,64,128]{3,2,1,0:T(8,128)S(1)} fusion(f32[8,7,8,64,128]{4,3,2,1,0:T(8,128)} %all-gather.2.cloned.1.call-done, f32[8]{0:T(128)S(1)} %select_reduce_fusion), kind=kLoop, calls=%fused_computation.25 | loop fusion | flops 6881280 | bytes 16515104 | tf_op jit(solution)/shard_map/reduce_sum | solution.py:150
  309.3 2.1 fusion.3
  315.6 17.0 %while.69 = (s32[]{:T(128)}, f32[64,128]{1,0:T(8,128)S(1)}, f32[9,64,128]{2,1,0:T(8,128)S(1)}, f32[7,64,128]{2,1,0:T(8,128)}, f32[7,9,64,128]{3,2,1,0:T(8,128)},...) while((s32[]{:T(128)}, f32[64,128]{1,0:T(8,128)S(1)}, ...), condition=%wide.region_3.4_spmd.clone, body=%wide.region_2.3_spmd.clone.sunk | while | flops 327683 | bytes 1475696 | solution.py:126
  316.3 1.8 bitcast_dynamic-update-slice_fusion.14
  318.7 1.8 bitcast_dynamic-update-slice_fusion.14
  321.1 1.8 bitcast_dynamic-update-slice_fusion.14
  323.6 1.8 bitcast_dynamic-update-slice_fusion.14
  326.0 1.8 bitcast_dynamic-update-slice_fusion.14
  328.4 1.8 bitcast_dynamic-update-slice_fusion.14
  330.8 1.8 bitcast_dynamic-update-slice_fusion.14
  334.2 18.1 %while.70 = (s32[]{:T(128)}, f32[9,64,128]{2,1,0:T(8,128)S(1)}, f32[7,9,64,128]{3,2,1,0:T(8,128)}, f32[7,9,64,128]{3,2,1,0:T(8,128)}, f32[7,64,128]{2,1,0:T(8,128)}, /*index=5*/s32[]{:T(128)}, s32[]{:T(128)}, s32[]{:T(128)}) while((s32[]{:T(128)}, f32[9,64,128]{2,1,0:T(8,128)S(1)}, f32[7,9,64,128]{3,2,1,0:T(8,128)}, ...), condition=%wide.region_5.6_spmd.clone, body=%wide.region_4.5_spmd.clone.sunk | while | flops 221188 | bytes 1278067 | solution.py:135
  335.0 1.8 bitcast_dynamic-update-slice_fusion.15
  337.6 1.8 bitcast_dynamic-update-slice_fusion.15
  340.1 1.8 bitcast_dynamic-update-slice_fusion.15
  342.7 1.8 bitcast_dynamic-update-slice_fusion.15
  345.3 1.8 bitcast_dynamic-update-slice_fusion.15
  347.9 1.8 bitcast_dynamic-update-slice_fusion.15
  350.5 1.8 bitcast_dynamic-update-slice_fusion.15
  354.1 2.7 collective-permute-start.3
  356.8 5.8 collective-permute-done.3
  364.5 3.0 stack.8
  367.5 6.9 %all-to-all-start = ((f32[16,1,10,64,128]{4,3,2,1,0:T(8,128)}), f32[16,1,10,64,128]{4,3,2,1,0:T(8,128)}, u32[]{:S(2)}, u32[]{:S(2)}) async-start(f32[16,1,10,64,128]{4,3,2,1,0:T(8,128)} %stack.8), calls=%async_computation | async-start | bytes 10485760 | tf_op jit(solution)/shard_map/all_to_all | solution.py:209
  375.6 114.8 %all-to-all-done = f32[16,1,10,64,128]{4,3,2,1,0:T(8,128)} async-done(((f32[16,1,10,64,128]{4,3,2,1,0:T(8,128)}), f32[16,1,10,64,128]{4,3,2,1,0:T(8,128)}, u32[]{:S(2)}, u32[]{:S(2)}) %all-to-all-start) | async-done | bytes 5242912 | tf_op jit(solution)/shard_map/all_to_all | solution.py:209
  490.4 4.4 slice.259
  494.8 2.5 slice_bitcast_fusion.1
  497.3 2.3 broadcast.406.clone
  499.6 49.7 %while.71 = (s32[]{:T(128)}, f32[64,128]{1,0:T(8,128)S(1)}, f32[7,64,128]{2,1,0:T(8,128)S(1)}, f32[16,64,128]{2,1,0:T(8,128)}, f32[16,7,64,128]{3,2,1,0:T(8,128)...) while((s32[]{:T(128)}, f32[64,128]{1,0:T(8,128)S(1)}, ...), condition=%wide.region_7.8_spmd.clone, body=%wide.region_6.7_spmd.clone.sunk | while | flops 262147 | bytes 1246328 | solution.py:126
  501.0 1.7 bitcast_dynamic-update-slice_fusion.17
  507.2 1.7 bitcast_dynamic-update-slice_fusion.17
  510.3 1.7 bitcast_dynamic-update-slice_fusion.17
  513.4 1.7 bitcast_dynamic-update-slice_fusion.17
  516.5 1.7 bitcast_dynamic-update-slice_fusion.17
  519.6 1.7 bitcast_dynamic-update-slice_fusion.17
  522.7 1.7 bitcast_dynamic-update-slice_fusion.17
  528.9 1.7 bitcast_dynamic-update-slice_fusion.17
  532.0 1.7 bitcast_dynamic-update-slice_fusion.17
  535.1 1.7 bitcast_dynamic-update-slice_fusion.17
  538.2 1.7 bitcast_dynamic-update-slice_fusion.17
  541.3 1.7 bitcast_dynamic-update-slice_fusion.17
  544.5 1.7 bitcast_dynamic-update-slice_fusion.17
  547.6 1.7 bitcast_dynamic-update-slice_fusion.17
  549.3 2.3 broadcast.406
  551.5 40.3 %while.72 = (s32[]{:T(128)}, f32[7,64,128]{2,1,0:T(8,128)S(1)}, f32[16,7,64,128]{3,2,1,0:T(8,128)}, f32[16,7,64,128]{3,2,1,0:T(8,128)}, f32[16,64,128]{2,1,0:T(8,128)}, /*index=5*/s32[]{:T(128)}, s32[]{:T(128)}, s32[]{:T(128)}) while((s32[]{:T(128)}, f32[7,64,128]{2,1,0:T(8,128)S(1)}, f32[16,7,64,128]{3,2,1,0:T(8,128)}, ...), condition=%wide.region_9.10_spmd.clone, body=%wide.region_8.9_spmd.clone.sunk | while | flops 172036 | bytes 1015923 | solution.py:135
  552.3 1.8 bitcast_dynamic-update-slice_fusion.18
  554.8 1.8 bitcast_dynamic-update-slice_fusion.18
  557.3 1.7 bitcast_dynamic-update-slice_fusion.18
  559.8 1.8 bitcast_dynamic-update-slice_fusion.18
  562.3 1.8 bitcast_dynamic-update-slice_fusion.18
  564.9 1.7 bitcast_dynamic-update-slice_fusion.18
  567.4 1.8 bitcast_dynamic-update-slice_fusion.18
  569.9 1.7 bitcast_dynamic-update-slice_fusion.18
  572.4 1.8 bitcast_dynamic-update-slice_fusion.18
  574.9 1.8 bitcast_dynamic-update-slice_fusion.18
  577.5 1.8 bitcast_dynamic-update-slice_fusion.18
  580.0 1.8 bitcast_dynamic-update-slice_fusion.18
  582.5 1.7 bitcast_dynamic-update-slice_fusion.18
  585.0 1.8 bitcast_dynamic-update-slice_fusion.18
  587.5 1.8 bitcast_dynamic-update-slice_fusion.18
  590.0 1.8 bitcast_dynamic-update-slice_fusion.18
  594.7 1.7 fusion.6
  (108 shorter events, 68.8 us)
Async XLA Ops:
  6.5 1.5 copy-start
  6.5 5.6 copy-start.4
  6.5 295.2 %all-gather.2.cloned.1.call-start = ((), (), s32[]{:S(2)}) async-start(), calls=%async_computation.1 | async-start | bytes 16515072 | tf_op jit(solution)/shard_map/all_gather | solution.py:146
  8.1 5.2 collective-permute-start
  11.7 5.3 collective-permute-start.1
  19.6 1.8 copy-start.1
  21.4 287.8 %collective-permute-start.2 = (f32[7,8,1,128]{3,2,1,0:T(1,128)S(1)}, f32[7,8,1,128]{3,2,1,0:T(1,128)S(1)}, u32[]{:S(2)}, u32[]{:S(2)}) collective-permute-start(f32[7,8,1,128]{3,2,1,0:T(1,128)S(1)} %slice.245), channel_id=1, source_target_pairs={{1,0},{0,1},{3,2},{2,3},{5,4},{4,5},{7,6},{6,7},{9,8},{8,9},{11,10... | collective-permute-start | bytes 86024 | tf_op jit(solution)/shard_map/ppermute | solution.py:34
  301.7 7.5 %copy-start.2 = (f32[7,8,64,128]{3,2,1,0:T(8,128)S(1)}, f32[7,8,64,128]{3,2,1,0:T(8,128)}, u32[]{:S(2)}) copy-start(f32[7,8,64,128]{3,2,1,0:T(8,128)} %copy-done.1) | copy-start | bytes 5505028
  311.4 1.2 copy-start.3
  354.1 8.5 %collective-permute-start.3 = (f32[9,64,128]{2,1,0:T(8,128)S(1)}, f32[9,64,128]{2,1,0:T(8,128)S(1)}, u32[]{:S(2)}, u32[]{:S(2)}) collective-permute-start(f32[9,64,128]{2,1,0:T(8,128)S(1)} %pad_maximum_fusion.4), channel_id=1, source_target_pairs={{2,0},{4,2},{6,4},{8,6},{10,8},{12,10},{14,12},{16,14},{18,16},{20... | collective-permute-start | bytes 884744 | tf_op jit(solution)/shard_map/ppermute | solution.py:40
  367.5 122.9 %all-to-all-start = ((f32[16,1,10,64,128]{4,3,2,1,0:T(8,128)}), f32[16,1,10,64,128]{4,3,2,1,0:T(8,128)}, u32[]{:S(2)}, u32[]{:S(2)}) async-start(f32[16,1,10,64,128]{4,3,2,1,0:T(8,128)} %stack.8), calls=%async_computation | async-start | bytes 10485760 | tf_op jit(solution)/shard_map/all_to_all | solution.py:209
Sparse Core Ops, SparseCore 0:
  9.1 292.5 all-gather.1
